TPU v7x, 32 devices: a whole 2x2x4 slice. The times are simulated.
32 devices in a mesh: grp: 4 (over y, x), shard: 8 (over z, core).
Axes of the slice: x: 2, y: 2, z: 4, core: 2. Of those that a mesh axis runs over, the one named last changes fastest.
Arguments:
- queries: bfloat16 [16, 32, 128], P('grp', 'shard'), may hold values from -7 to 7
- paged_key_cache: bfloat16 [2048, 8, 64, 128], P(('grp', 'shard')), may hold values from -8 to 8
- paged_value_cache: bfloat16 [2048, 8, 64, 128], P(('grp', 'shard')), may hold values from -6 to 6
- summary_keys: bfloat16 [8, 2048, 128], P(None, ('grp', 'shard')), may hold values from -8 to 8
- summary_values: bfloat16 [8, 2048, 128], P(None, ('grp', 'shard')), may hold values from -6 to 6
- gate_logits: float32 [2, 16, 32], P(None, 'grp', 'shard'), may hold values from -6 to 6
- block_group_row: int32 [16, 128], P('grp'), may hold values from 0 to 511, as said below
- picked: int32 [8, 16, 8], P(None, 'grp'), may hold values from 0 to 127, as said below
Outputs:
- attention: float32 [16, 32, 128], P('grp', 'shard')
- retrieval_counts: float32 [128], replicated
Inputs may be any that keep to these rules, and one draw needn't show every extreme that they name: block_group_row is one to one within each group. For slot = block_group_row[b, k], slot // 64 is the index along shard of the device that stores block k of sequence b and slot % 64 its place there; every device stores 16 blocks of each sequence of its group, the sequence numbered s within the group in places s * 16 to s * 16 + 15. picked[g, b, :] names 8 blocks of sequence b stored on 8 different devices. For one key head and one group, take an aligned run of r sequences of the group (r dividing 4): among all their picks at most min(r, 8) are stored on any one device; for r = 4 some device stores exactly min(4, 8) of them.
All inputs are finite; a program needn't handle non-finite values.
Results may differ from a plain program's by a relative error of at most 0.006.
Values may be sent and summed in bfloat16 or wider, within the bound.
No kernel may reach another device: no remote copies, remote signals or barrier semaphores. Data moves between devices by JAX's collectives and lax.ppermute only.
A program may use at most 128 MiB of HBM per device.

v0:
```python
import functools

import jax
import jax.numpy as jnp
from jax import lax
from jax.experimental import pallas as pl
from jax.experimental.pallas import tpu as pltpu
from jax.sharding import PartitionSpec as P


VERY_NEGATIVE = -1e30
VMEM = pltpu.VMEM
SMEM = pltpu.SMEM
LIMIT = 4 * 1024 * 1024


def fetch_kernel(rows_hbm, picked_hbm, keys_hbm, values_hbm, keys_out, values_out, counts_out, *refs, slots_here, blocks_each):
    valid_out = refs[0] if len(refs) == 9 else None
    rows_ref, picked_ref, picked_tile, rows_sem, picked_sem, tile_sem, key_sem, value_sem = refs[-8:]
    copies = [
        pltpu.make_async_copy(rows_hbm, rows_ref, rows_sem),
        pltpu.make_async_copy(picked_hbm, picked_ref, picked_sem),
        pltpu.make_async_copy(picked_hbm, picked_tile, tile_sem),
    ]
    for copy in copies:
        copy.start()
    key_heads, sequences, picks = picked_ref.shape
    first = lax.axis_index("shard") * slots_here
    for copy in copies[:2]:
        copy.wait()
    for head in range(key_heads):
        for sequence in range(sequences):
            place = jnp.int32(sequence * blocks_each)
            found = jnp.int32(0)
            for pick in range(picks):
                slot = rows_ref[sequence, picked_ref[head, sequence, pick]] - first
                here = (slot >= 0) & (slot < slots_here)
                place = jnp.where(here, slot, place)
                found = jnp.where(here, 1, found)
            if valid_out is not None:
                valid_out[head, sequence] = found
            pltpu.make_async_copy(keys_hbm.at[place, head], keys_out.at[head, sequence], key_sem).start()
            pltpu.make_async_copy(values_hbm.at[place, head], values_out.at[head, sequence], value_sem).start()
    copies[2].wait()
    told_rows, width = counts_out.shape
    counts = []
    for row in range(told_rows):
        sums = [jnp.zeros((sequences, width), jnp.float32) for _ in range(2)]
        if row * width < rows_ref.shape[1]:
            block_ids = lax.broadcasted_iota(jnp.int32, (sequences, width), 1) + row * width
            for head in range(key_heads):
                tile = picked_tile[head]
                for pick in range(picks):
                    sums[pick % 2] += jnp.where(tile[:, pick : pick + 1] == block_ids, 1.0, 0.0)
        counts.append(jnp.sum(sums[0] + sums[1], axis=0, keepdims=True))
    counts_out[...] = jnp.concatenate(counts, axis=0).astype(jnp.bfloat16)
    pltpu.make_async_copy(keys_out, keys_out, key_sem).wait()
    pltpu.make_async_copy(values_out, values_out, value_sem).wait()


def fetch(block_group_row, picked, keys, values, always):
    key_heads, sequences, _ = picked.shape
    slots_here, _, tokens, width = keys.shape
    gathered = jax.ShapeDtypeStruct((key_heads, sequences, tokens, width), keys.dtype)
    told_rows = -(-block_group_row.shape[1] // (8 * width)) * 8
    nbytes = 2 * key_heads * sequences * tokens * width * 2
    out_shape = [gathered, gathered, jax.ShapeDtypeStruct((told_rows, width), jnp.bfloat16)]
    out_specs = [pl.BlockSpec(memory_space=VMEM)] * 3
    if not always:
        out_shape.append(jax.ShapeDtypeStruct((key_heads, sequences), jnp.int32))
        out_specs.append(pl.BlockSpec(memory_space=SMEM))
    out = pl.pallas_call(
        functools.partial(fetch_kernel, slots_here=slots_here, blocks_each=slots_here // sequences),
        out_shape=out_shape,
        in_specs=[pl.BlockSpec(memory_space=pltpu.HBM)] * 4,
        out_specs=out_specs,
        scratch_shapes=[
            SMEM(block_group_row.shape, jnp.int32),
            SMEM(picked.shape, jnp.int32),
            VMEM(picked.shape, jnp.int32),
        ]
        + [pltpu.SemaphoreType.DMA] * 5,
        cost_estimate=pl.CostEstimate(flops=0, transcendentals=0, bytes_accessed=2 * nbytes),
        compiler_params=pltpu.CompilerParams(vmem_limit_bytes=LIMIT),
        name="fetch",
    )(*(pltpu.with_memory_space_constraint(x, pltpu.HBM) for x in (block_group_row, picked, keys, values)))
    return out[0], out[1], out[2], None if always else out[3]


def split3(x):
    high = x.astype(jnp.bfloat16).astype(jnp.float32)
    rest = x - high
    middle = rest.astype(jnp.bfloat16).astype(jnp.float32)
    return high, middle, rest - middle


def attend_part(query, keys, values, usable, present):
    scaling = query.shape[-1] ** -0.5
    scores = lax.dot_general(query, keys, (((1,), (1,)), ((), ())), preferred_element_type=jnp.float32) * scaling
    scores = jnp.where(usable, scores, VERY_NEGATIVE)
    highest = jnp.max(scores, axis=-1, keepdims=True)
    exponent = jnp.exp(scores - highest)
    if present is not None:
        exponent = jnp.where(present, exponent, 0.0)
    total = jnp.sum(exponent, axis=-1, keepdims=True)
    numerator = lax.dot_general(
        exponent.astype(jnp.bfloat16), values, (((1,), (0,)), ((), ())), preferred_element_type=jnp.float32
    )
    return highest, total, numerator


def usable_for(rows, columns, each, heads_here, sequences):
    row = lax.broadcasted_iota(jnp.int32, (rows, columns), 0)
    column = lax.broadcasted_iota(jnp.int32, (rows, columns), 1)
    return (row // heads_here) % sequences == column // each


def partial_kernel(query_ref, keys_ref, values_ref, summary_keys_ref, summary_values_ref, told_ref, *refs, heads_here):
    valid_ref = refs[0] if len(refs) == 2 else None
    out_ref = refs[-1]
    key_heads, rows, width = query_ref.shape
    _, sequences, tokens, _ = keys_ref.shape
    slots = summary_keys_ref.shape[1]
    shards, sent_rows, _ = out_ref.shape
    told_rows = told_ref.shape[0]
    out_rows = (sent_rows - told_rows) // 3
    per_head = rows // out_rows

    usable_block = usable_for(rows, sequences * tokens, tokens, heads_here, sequences)
    usable_summary = usable_for(rows, slots, slots // sequences, heads_here, sequences)
    lane = lax.broadcasted_iota(jnp.int32, (rows, width), 1)
    for shard in range(shards):
        out_ref[shard, 3 * out_rows :, :] = told_ref[...]
    for head in range(key_heads):
        query = query_ref[head]
        present = None
        usable = usable_block
        if valid_ref is not None:
            column = lax.broadcasted_iota(jnp.int32, (rows, sequences * tokens), 1) // tokens
            flag = jnp.zeros((rows, sequences * tokens), jnp.int32)
            for sequence in range(sequences):
                flag = jnp.where(column == sequence, valid_ref[head, sequence], flag)
            usable = usable_block & (flag > 0)
            present = usable
        keys = keys_ref[head].reshape(sequences * tokens, width)
        values = values_ref[head].reshape(sequences * tokens, width)
        top_s, sum_s, num_s = attend_part(query, keys, values, usable, present)
        top_l, sum_l, num_l = attend_part(query, summary_keys_ref[head], summary_values_ref[head], usable_summary, None)
        stats = jnp.zeros((rows, width), jnp.float32)
        at = 0
        for value in (top_l, sum_l, top_s, sum_s):
            for term in split3(value):
                stats = jnp.where(lane == at, term, stats)
                at += 1
        for part in range(per_head):
            here = slice(part * out_rows, (part + 1) * out_rows)
            target = head * per_head + part
            for i, piece in enumerate((num_l, num_s, stats)):
                out_ref[target, i * out_rows : (i + 1) * out_rows, :] = piece[here].astype(jnp.bfloat16)


def partials(query, keys, values, summary_keys, summary_values, told, valid, shards, heads_here):
    key_heads, rows, width = query.shape
    out_rows = key_heads * rows // shards
    operands = [query, keys, values, summary_keys, summary_values, told]
    in_specs = [pl.BlockSpec(memory_space=VMEM)] * 6
    if valid is not None:
        operands.append(valid)
        in_specs.append(pl.BlockSpec(memory_space=SMEM))
    return pl.pallas_call(
        functools.partial(partial_kernel, heads_here=heads_here),
        out_shape=jax.ShapeDtypeStruct((shards, 3 * out_rows + told.shape[0], width), jnp.bfloat16),
        in_specs=in_specs,
        out_specs=pl.BlockSpec(memory_space=VMEM),
        compiler_params=pltpu.CompilerParams(vmem_limit_bytes=LIMIT),
        name="partials",
    )(*operands)


def merge_kernel(parts_ref, gates_ref, counts_ref, out_ref, counts_out, *, tellers):
    sources, sent_rows, width = parts_ref.shape
    told_rows = counts_ref.shape[0]
    rows = (sent_rows - told_rows) // 3
    _, sequences, heads_here = gates_ref.shape
    counts = counts_ref[...].astype(jnp.float32)
    for teller in range(tellers):
        counts += parts_ref[teller, 3 * rows :, :].astype(jnp.float32)
    counts_out[...] = counts[: counts_out.shape[0]]
    stats = []
    for source in range(sources):
        raw = parts_ref[source, 2 * rows : 3 * rows, :].astype(jnp.float32)
        stats.append([raw[:, i : i + 1] + raw[:, i + 1 : i + 2] + raw[:, i + 2 : i + 3] for i in (0, 3, 6, 9)])
    row = lax.broadcasted_iota(jnp.int32, (rows, heads_here), 0)
    column = lax.broadcasted_iota(jnp.int32, (rows, heads_here), 1)
    result = None
    for branch in range(2):
        highest = functools.reduce(jnp.maximum, [s[2 * branch] for s in stats])
        total = jnp.zeros((rows, 1), jnp.float32)
        numerator = jnp.zeros((rows, width), jnp.float32)
        for source in range(sources):
            weight = jnp.exp(stats[source][2 * branch] - highest)
            total += weight * stats[source][2 * branch + 1]
            numerator += weight * parts_ref[source, branch * rows : (branch + 1) * rows, :].astype(jnp.float32)
        gate = 1.0 / (1.0 + jnp.exp(-gates_ref[branch]))
        spread = jnp.zeros((rows, heads_here), jnp.float32)
        for sequence in range(sequences):
            spread = jnp.where(row // heads_here == sequence, gate[sequence : sequence + 1, :], spread)
        spread = jnp.sum(jnp.where(column == row % heads_here, spread, 0.0), axis=1, keepdims=True)
        term = numerator * (spread / total)
        result = term if result is None else result + term
    out_ref[...] = result


def merge(parts, gates, counts, count_rows, tellers):
    rows = (parts.shape[1] - counts.shape[0]) // 3
    width = parts.shape[2]
    return pl.pallas_call(
        functools.partial(merge_kernel, tellers=tellers),
        out_shape=(
            jax.ShapeDtypeStruct((rows, width), jnp.float32),
            jax.ShapeDtypeStruct((count_rows, width), jnp.float32),
        ),
        in_specs=[pl.BlockSpec(memory_space=VMEM)] * 3,
        out_specs=(pl.BlockSpec(memory_space=VMEM),) * 2,
        compiler_params=pltpu.CompilerParams(vmem_limit_bytes=LIMIT),
        name="merge",
    )(parts, gates, counts)


def half_kernel(query_ref, keys_ref, values_ref, summary_keys_ref, summary_values_ref, out_ref, *, heads_here, flip):
    chips, rows, width = query_ref.shape
    _, sequences, tokens, _ = keys_ref.shape
    slots = summary_keys_ref.shape[1]
    me = lax.axis_index("shard")
    chip, core = me // 2, me % 2
    if flip:
        core = 1 - core
    usable_block = usable_for(rows, sequences * tokens, tokens, heads_here, sequences)
    usable_summary = usable_for(rows, slots, slots // sequences, heads_here, sequences)
    lane = lax.broadcasted_iota(jnp.int32, (rows, width), 1)
    for step in range(chips):
        head = lax.rem(chip + (chips - step), chips) * 2 + core
        query = query_ref[step]
        keys = keys_ref[head].reshape(sequences * tokens, width)
        values = values_ref[head].reshape(sequences * tokens, width)
        top_s, sum_s, num_s = attend_part(query, keys, values, usable_block, None)
        top_l, sum_l, num_l = attend_part(query, summary_keys_ref[head], summary_values_ref[head], usable_summary, None)
        stats = jnp.where(lane == 0, top_l, jnp.where(lane == 1, sum_l, jnp.where(lane == 2, top_s, sum_s)))
        out_ref[step, :rows, :] = num_l
        out_ref[step, rows : 2 * rows, :] = num_s
        out_ref[step, 2 * rows :, :] = stats


def half(query, keys, values, summary_keys, summary_values, heads_here, flip):
    chips, rows, width = query.shape
    return pl.pallas_call(
        functools.partial(half_kernel, heads_here=heads_here, flip=flip),
        out_shape=jax.ShapeDtypeStruct((chips, 3 * rows, width), jnp.float32),
        in_specs=[pl.BlockSpec(memory_space=VMEM)] * 5,
        out_specs=pl.BlockSpec(memory_space=VMEM),
        cost_estimate=pl.CostEstimate(flops=10**8, transcendentals=10**5, bytes_accessed=10**6),
        compiler_params=pltpu.CompilerParams(vmem_limit_bytes=LIMIT),
        name="other_half" if flip else "own_half",
    )(query, keys, values, summary_keys, summary_values)


def join_kernel(own_ref, other_ref, told_ref, *out_refs, silent):
    chips, rows3, width = own_ref.shape
    told = jnp.where(lax.axis_index("shard") // 2 == silent, 0.0, told_ref[...].astype(jnp.float32)).astype(jnp.bfloat16)
    rows = rows3 // 3
    lane = lax.broadcasted_iota(jnp.int32, (rows, width), 1)
    for step in range(chips):
        out_ref = out_refs[step]
        own_stats = own_ref[step, 2 * rows :, :]
        other_stats = other_ref[step, 2 * rows :, :]
        stats = jnp.zeros((rows, width), jnp.float32)
        at = 0
        for branch in range(2):
            here = slice(branch * rows, (branch + 1) * rows)
            own_top, other_top = own_stats[:, 2 * branch : 2 * branch + 1], other_stats[:, 2 * branch : 2 * branch + 1]
            own_sum, other_sum = own_stats[:, 2 * branch + 1 : 2 * branch + 2], other_stats[:, 2 * branch + 1 : 2 * branch + 2]
            highest = jnp.maximum(own_top, other_top)
            own_weight, other_weight = jnp.exp(own_top - highest), jnp.exp(other_top - highest)
            numerator = own_weight * own_ref[step, here, :] + other_weight * other_ref[step, here, :]
            out_ref[here, :] = numerator.astype(jnp.bfloat16)
            for value in (highest, own_weight * own_sum + other_weight * other_sum):
                for term in split3(value):
                    stats = jnp.where(lane == at, term, stats)
                    at += 1
        out_ref[2 * rows : 3 * rows, :] = stats.astype(jnp.bfloat16)
        out_ref[3 * rows :, :] = told


def join(own, other, told, silent):
    chips, rows3, width = own.shape
    shape = jax.ShapeDtypeStruct((rows3 + told.shape[0], width), jnp.bfloat16)
    return pl.pallas_call(
        functools.partial(join_kernel, silent=silent),
        out_shape=[shape] * chips,
        in_specs=[pl.BlockSpec(memory_space=VMEM)] * 3,
        out_specs=[pl.BlockSpec(memory_space=VMEM)] * chips,
        compiler_params=pltpu.CompilerParams(vmem_limit_bytes=LIMIT),
        name="join",
    )(own, other, told)


def finish_kernel(*refs):
    *part_refs, gates_ref, counts_ref, out_ref, counts_out = refs
    rows, width = out_ref.shape
    _, sequences, heads_here = gates_ref.shape
    counts = counts_ref[...].astype(jnp.float32) + sum(ref[3 * rows :, :].astype(jnp.float32) for ref in part_refs)
    counts_out[...] = counts[: counts_out.shape[0]]
    row = lax.broadcasted_iota(jnp.int32, (rows, heads_here), 0)
    column = lax.broadcasted_iota(jnp.int32, (rows, heads_here), 1)
    stats = []
    for ref in part_refs:
        raw = ref[2 * rows : 3 * rows, :].astype(jnp.float32)
        stats.append([raw[:, i : i + 1] + raw[:, i + 1 : i + 2] + raw[:, i + 2 : i + 3] for i in (0, 3, 6, 9)])
    result = jnp.zeros((rows, width), jnp.float32)
    for branch in range(2):
        highest = functools.reduce(jnp.maximum, [s[2 * branch] for s in stats])
        weights = [jnp.exp(s[2 * branch] - highest) for s in stats]
        total = sum(weight * s[2 * branch + 1] for weight, s in zip(weights, stats))
        here = slice(branch * rows, (branch + 1) * rows)
        numerator = sum(weight * ref[here, :].astype(jnp.float32) for weight, ref in zip(weights, part_refs))
        gate = 1.0 / (1.0 + jnp.exp(-gates_ref[branch]))
        spread = jnp.zeros((rows, heads_here), jnp.float32)
        for sequence in range(sequences):
            spread = jnp.where(row // heads_here == sequence, gate[sequence : sequence + 1, :], spread)
        spread = jnp.sum(jnp.where(column == row % heads_here, spread, 0.0), axis=1, keepdims=True)
        result += numerator * (spread / total)
    out_ref[...] = result


def finish(parts, gates, counts, rows, count_rows):
    width = parts[0].shape[1]
    return pl.pallas_call(
        finish_kernel,
        out_shape=(
            jax.ShapeDtypeStruct((rows, width), jnp.float32),
            jax.ShapeDtypeStruct((count_rows, width), jnp.float32),
        ),
        in_specs=[pl.BlockSpec(memory_space=VMEM)] * (len(parts) + 2),
        out_specs=(pl.BlockSpec(memory_space=VMEM),) * 2,
        compiler_params=pltpu.CompilerParams(vmem_limit_bytes=LIMIT),
        name="finish",
    )(*parts, gates, counts)


def by_chips(queries, keys_cache, values_cache, summary_keys, summary_values, gate_logits, block_group_row, picked):
    groups, shards = lax.axis_size("grp"), lax.axis_size("shard")
    chips = shards // 2
    sequences, heads_here, width = queries.shape
    blocks = block_group_row.shape[1]
    rows = sequences * heads_here

    def shift(step):
        return [(s, (s // 2 + step) % chips * 2 + s % 2) for s in range(shards)]

    partner = [(s, s ^ 1) for s in range(shards)]
    mine = queries.reshape(rows, width)
    arrived = []
    for step in range(1, chips):
        arrived.append(lax.ppermute(mine, "shard", shift(step)))
    keys, values, counts, _ = fetch(block_group_row, picked, keys_cache, values_cache, True)
    offsets = [groups - 1 if chip == groups - 1 else chip % (groups - 2) + 1 for chip in range(chips)] if groups > 2 else [1] * chips
    pairs = [
        ((group ^ offsets[shard // 2]) * shards + shard, group * shards + shard)
        for group in range(groups)
        for shard in range(shards)
    ]
    told = lax.ppermute(counts, ("grp", "shard"), pairs)
    own_query = jnp.stack([mine] + arrived)
    other_query = lax.ppermute(own_query, "shard", partner)
    own = half(own_query, keys, values, summary_keys, summary_values, heads_here, False)
    other = half(other_query, keys, values, summary_keys, summary_values, heads_here, True)
    other = lax.ppermute(other, "shard", partner)
    parts = list(join(own, other, told, groups - 2))
    for step in range(1, chips):
        parts[step] = lax.ppermute(parts[step], "shard", shift(-step))
    attention, retrieval_counts = finish(parts, gate_logits, counts, rows, blocks // width)
    return attention.reshape(sequences, heads_here, width), retrieval_counts.reshape(-1)


def body(
    queries,
    paged_key_cache,
    paged_value_cache,
    summary_keys,
    summary_values,
    gate_logits,
    block_group_row,
    picked,
):
    groups, shards = lax.axis_size("grp"), lax.axis_size("shard")
    sequences, heads_here, width = queries.shape
    key_heads, _, picks = picked.shape
    blocks = block_group_row.shape[1]
    rows = sequences * heads_here
    always = shards == picks
    if shards == key_heads == picks and shards == 2 * groups and groups & (groups - 1) == 0:
        return by_chips(
            queries, paged_key_cache, paged_value_cache, summary_keys, summary_values, gate_logits, block_group_row, picked
        )

    keys, values, counts, valid = fetch(block_group_row, picked, paged_key_cache, paged_value_cache, always)
    tellers = groups - 1
    pairs = [
        ((group + 1 + shard) % groups * shards + shard, group * shards + shard)
        for group in range(groups)
        for shard in range(tellers)
    ]
    told = lax.ppermute(counts, ("grp", "shard"), pairs)

    copies = jnp.broadcast_to(queries.reshape(1, rows, width), (shards, rows, width))
    everyone = lax.all_to_all(copies, "shard", split_axis=0, concat_axis=0, tiled=True)
    everyone = everyone.reshape(key_heads, shards * rows // key_heads, width)
    outgoing = partials(everyone, keys, values, summary_keys, summary_values, told, valid, shards, heads_here)
    incoming = lax.all_to_all(outgoing, "shard", split_axis=0, concat_axis=0, tiled=True)
    attention, retrieval_counts = merge(incoming, gate_logits, counts, blocks // width, tellers)
    return attention.reshape(sequences, heads_here, width), retrieval_counts.reshape(-1)


def solution(mesh):
    placed = (
        P("grp", "shard", None),
        P(("grp", "shard"), None, None, None),
        P(("grp", "shard"), None, None, None),
        P(None, ("grp", "shard"), None),
        P(None, ("grp", "shard"), None),
        P(None, "grp", "shard"),
        P("grp", None),
        P(None, "grp", None),
    )
    return jax.shard_map(
        body, mesh=mesh, in_specs=placed, out_specs=(P("grp", "shard", None), P()), check_vma=False
    )
```

profile of v0, /device:TPU:0, one launch (start us, length us, event | category | flops | bytes accessed | tf_op | source)
XLA Modules:
  0.0 28.6 jit_solution(15452980165179477026)
XLA Ops:
  0.6 5.1 %collective-permute-start.2 = (bf16[16,128]{1,0:T(8,128)(2,1)}, bf16[16,128]{1,0:T(8,128)(2,1)S(1)}, u32[]{:S(2)}, u32[]{:S(2)}) collective-permute-start(bf16[16,128]{1,0:T(8,128)(2,1)} %bitcast.7), channel_id=1, source_target_pairs={{0,6},{1,7},{2,0},{3,1},{4,2},{5,3},{6,4},{7,5},{8,14},{9,15},{10,... | collective-permute-start | bytes 12296 | tf_op jit(solution)/shard_map/ppermute | solution.py:364
  5.8 0.0 collective-permute-start.1
  5.8 1.0 %collective-permute-start = (bf16[16,128]{1,0:T(8,128)(2,1)}, bf16[16,128]{1,0:T(8,128)(2,1)S(1)}, u32[]{:S(2)}, u32[]{:S(2)}) collective-permute-start(bf16[16,128]{1,0:T(8,128)(2,1)} %bitcast.9), channel_id=1, source_target_pairs={{0,2},{1,3},{2,4},{3,5},{4,6},{5,7},{6,0},{7,1},{8,10},{9,11},{10,... | collective-permute-start | bytes 12296 | tf_op jit(solution)/shard_map/ppermute | solution.py:364
  6.8 0.5 %collective-permute-done.2 = bf16[16,128]{1,0:T(8,128)(2,1)S(1)} collective-permute-done((bf16[16,128]{1,0:T(8,128)(2,1)}, bf16[16,128]{1,0:T(8,128)(2,1)S(1)}, u32[]{:S(2)}, u32[]{:S(2)}) %collective-permute-start.2) | collective-permute-done | bytes 4128 | tf_op jit(solution)/shard_map/ppermute | solution.py:364
  7.3 3.2 %collective-permute-done.1 = bf16[16,128]{1,0:T(8,128)(2,1)S(1)} collective-permute-done((bf16[16,128]{1,0:T(8,128)(2,1)}, bf16[16,128]{1,0:T(8,128)(2,1)S(1)}, u32[]{:S(2)}, u32[]{:S(2)}) %collective-permute-start.1) | collective-permute-done | bytes 4128 | tf_op jit(solution)/shard_map/ppermute | solution.py:364
  10.5 0.9 %collective-permute-done = bf16[16,128]{1,0:T(8,128)(2,1)S(1)} collective-permute-done((bf16[16,128]{1,0:T(8,128)(2,1)}, bf16[16,128]{1,0:T(8,128)(2,1)S(1)}, u32[]{:S(2)}, u32[]{:S(2)}) %collective-permute-start) | collective-permute-done | bytes 4128 | tf_op jit(solution)/shard_map/ppermute | solution.py:364
  11.4 0.7 %pad_maximum_fusion.query_ref = bf16[4,16,128]{2,1,0:T(8,128)(2,1)S(1)} fusion(bf16[1,16,128]{2,1,0:T(8,128)(2,1)S(1)} %bitcast.11, bf16[1,16,128]{2,1,0:T(8,128)(2,1)S(1)} %bitcast.12, bf16[1,16,128]{2,1,0:T(8,128)(2,1)S(1)} %bitcast.13, bf16[1,16,128]{2,1,0:T(8,128)(2,1)} %bitcast.10), kind=kLoop, calls=%fused_computation | loop fusion | flops 24576 | bytes 32768 | tf_op jit(solution)/shard_map/stack | solution.py:373
  12.1 0.0 copy-start
  12.1 0.0 copy-start.1
  12.1 0.0 copy-start.2
  12.1 0.1 collective-permute-start.3
  12.2 2.8 %fetch.1 = (bf16[8,4,64,128]{3,2,1,0:T(8,128)(2,1)S(1)}, bf16[8,4,64,128]{3,2,1,0:T(8,128)(2,1)S(1)}, bf16[8,128]{1,0:T(8,128)(2,1)S(1)}) custom-call(s32[4,128]{1,0:T(4,128)} %rows_hbm.1, s32[8,4,8]{2,1,0:T(4,128)} %picked_hbm.1, bf16[64,8,64,128]{3,2,1,0:T(8,128)(2,1)} %keys_hbm.1, bf16[64,8,64,128]{3,2,1,0:T(8,128)(2,1)} %values_hbm.1), custom_call_target="tpu_custom_call" | custom-call | bytes 2097152 | tf_op jit(solution)/shard_map/fetch/pallas_call | solution.py:72
  15.0 0.0 collective-permute-done.3.query_ref
  15.0 0.0 copy-done
  15.0 0.0 copy-done.1
  15.0 1.3 %other_half.1 = f32[4,48,128]{2,1,0:T(8,128)S(1)} custom-call(bf16[4,16,128]{2,1,0:T(8,128)(2,1)S(1)} %collective-permute-done.3.query_ref, bf16[8,4,64,128]{3,2,1,0:T(8,128)(2,1)S(1)} %get-tuple-element.11.keys_ref, bf16[8,4,64,128]{3,2,1,0:T(8,128)(2,1)S(1)} %get-tuple-element.12.values_ref, bf16[8,64,128]{2,1,0:T(8,128)(2,1)S(1)} %copy-done, ...), custom_call_target="tpu_custom_call" | custom-call | flops 100000000 | bytes 1000000 | tf_op jit(solution)/shard_map/other_half/pallas_call | solution.py:256
  16.4 0.4 %collective-permute-start.4 = (f32[4,48,128]{2,1,0:T(8,128)S(1)}, f32[4,48,128]{2,1,0:T(8,128)S(1)}, u32[]{:S(2)}, u32[]{:S(2)}) collective-permute-start(f32[4,48,128]{2,1,0:T(8,128)S(1)} %other_half.1), channel_id=1, source_target_pairs={{0,1},{1,0},{2,3},{3,2},{4,5},{5,4},{6,7},{7,6},{8,9},{9,8},{10,11... | collective-permute-start | bytes 294920 | tf_op jit(solution)/shard_map/ppermute | solution.py:377
  16.7 1.5 %collective-permute-start.5 = (bf16[8,128]{1,0:T(8,128)(2,1)S(1)}, bf16[8,128]{1,0:T(8,128)(2,1)S(1)}, u32[]{:S(2)}, u32[]{:S(2)}) collective-permute-start(bf16[8,128]{1,0:T(8,128)(2,1)S(1)} %get-tuple-element.13.refs_5_), channel_id=1, source_target_pairs={{8,0},{9,1},{18,2},{19,3},{12,4},{13,5},{30,6},{31,7},{0,8},{1,9},... | collective-permute-start | bytes 6152 | tf_op jit(solution)/shard_map/ppermute | solution.py:372
  18.2 1.3 %own_half.1.own_ref = f32[4,48,128]{2,1,0:T(8,128)S(1)} custom-call(bf16[4,16,128]{2,1,0:T(8,128)(2,1)S(1)} %pad_maximum_fusion.query_ref, bf16[8,4,64,128]{3,2,1,0:T(8,128)(2,1)S(1)} %get-tuple-element.11.keys_ref, bf16[8,4,64,128]{3,2,1,0:T(8,128)(2,1)S(1)} %get-tuple-element.12.values_ref, bf16[8,64,128]{2,1,0:T(8,128)(2,1)S(1)} %copy-done, ...), custom_call_target="tpu_custom_call" | custom-call | flops 100000000 | bytes 1000000 | tf_op jit(solution)/shard_map/own_half/pallas_call | solution.py:256
  19.6 0.8 %collective-permute-done.5.told_ref = bf16[8,128]{1,0:T(8,128)(2,1)S(1)} collective-permute-done((bf16[8,128]{1,0:T(8,128)(2,1)S(1)}, bf16[8,128]{1,0:T(8,128)(2,1)S(1)}, u32[]{:S(2)}, u32[]{:S(2)}) %collective-permute-start.5) | collective-permute-done | bytes 2080 | tf_op jit(solution)/shard_map/ppermute | solution.py:372
  20.3 0.0 collective-permute-done.4.other_ref
  20.3 0.3 %join.1 = (bf16[56,128]{1,0:T(8,128)(2,1)S(1)}, bf16[56,128]{1,0:T(8,128)(2,1)S(1)}, bf16[56,128]{1,0:T(8,128)(2,1)S(1)}, bf16[56,128]{1,0:T(8,128)(2,1)S(1)}) custom-call(f32[4,48,128]{2,1,0:T(8,128)S(1)} %own_half.1.own_ref, f32[4,48,128]{2,1,0:T(8,128)S(1)} %collective-permute-done.4.other_ref, bf16[8,128]{1,0:T(8,128)(2,1)S(1)} %collective-permute-done.5.told_ref), custom_call_target="tpu_custom_call" | custom-call | tf_op jit(solution)/shard_map/join/pallas_call | solution.py:297
  20.7 1.5 %collective-permute-start.6 = (bf16[56,128]{1,0:T(8,128)(2,1)S(1)}, bf16[56,128]{1,0:T(8,128)(2,1)S(1)}, u32[]{:S(2)}, u32[]{:S(2)}) collective-permute-start(bf16[56,128]{1,0:T(8,128)(2,1)S(1)} %get-tuple-element.15), channel_id=1, source_target_pairs={{0,6},{1,7},{2,0},{3,1},{4,2},{5,3},{6,4},{7,5},{8,14},{9,15},{10,... | collective-permute-start | bytes 43016 | tf_op jit(solution)/shard_map/ppermute | solution.py:380
  22.2 0.0 collective-permute-start.7
  22.2 1.7 %collective-permute-start.8 = (bf16[56,128]{1,0:T(8,128)(2,1)S(1)}, bf16[56,128]{1,0:T(8,128)(2,1)S(1)}, u32[]{:S(2)}, u32[]{:S(2)}) collective-permute-start(bf16[56,128]{1,0:T(8,128)(2,1)S(1)} %get-tuple-element.17), channel_id=1, source_target_pairs={{0,2},{1,3},{2,4},{3,5},{4,6},{5,7},{6,0},{7,1},{8,10},{9,11},{10,... | collective-permute-start | bytes 43016 | tf_op jit(solution)/shard_map/ppermute | solution.py:380
  23.9 0.6 %collective-permute-done.6.refs_1_ = bf16[56,128]{1,0:T(8,128)(2,1)S(1)} collective-permute-done((bf16[56,128]{1,0:T(8,128)(2,1)S(1)}, bf16[56,128]{1,0:T(8,128)(2,1)S(1)}, u32[]{:S(2)}, u32[]{:S(2)}) %collective-permute-start.6) | collective-permute-done | bytes 14368 | tf_op jit(solution)/shard_map/ppermute | solution.py:380
  24.4 2.5 %collective-permute-done.7.refs_2_ = bf16[56,128]{1,0:T(8,128)(2,1)S(1)} collective-permute-done((bf16[56,128]{1,0:T(8,128)(2,1)S(1)}, bf16[56,128]{1,0:T(8,128)(2,1)S(1)}, u32[]{:S(2)}, u32[]{:S(2)}) %collective-permute-start.7) | collective-permute-done | bytes 14368 | tf_op jit(solution)/shard_map/ppermute | solution.py:380
  26.9 0.8 %collective-permute-done.8.refs_3_ = bf16[56,128]{1,0:T(8,128)(2,1)S(1)} collective-permute-done((bf16[56,128]{1,0:T(8,128)(2,1)S(1)}, bf16[56,128]{1,0:T(8,128)(2,1)S(1)}, u32[]{:S(2)}, u32[]{:S(2)}) %collective-permute-start.8) | collective-permute-done | bytes 14368 | tf_op jit(solution)/shard_map/ppermute | solution.py:380
  27.7 0.0 copy-done.2
  27.7 0.8 %finish.1 = (f32[16,128]{1,0:T(8,128)}, f32[1,128]{1,0:T(1,128)}) custom-call(bf16[56,128]{1,0:T(8,128)(2,1)S(1)} %get-tuple-element.14.refs_0_, bf16[56,128]{1,0:T(8,128)(2,1)S(1)} %collective-permute-done.6.refs_1_, bf16[56,128]{1,0:T(8,128)(2,1)S(1)} %collective-permute-done.7.refs_2_, bf16[56,128]{1,0:T(8,128)(2,1)S(1)} %collective-permute-done.8.refs_3_, ...), custom_call_target="tpu_custom_call" | custom-call | tf_op jit(solution)/shard_map/finish/pallas_call | solution.py:337
Async XLA Ops:
  0.6 6.7 %collective-permute-start.2 = (bf16[16,128]{1,0:T(8,128)(2,1)}, bf16[16,128]{1,0:T(8,128)(2,1)S(1)}, u32[]{:S(2)}, u32[]{:S(2)}) collective-permute-start(bf16[16,128]{1,0:T(8,128)(2,1)} %bitcast.7), channel_id=1, source_target_pairs={{0,6},{1,7},{2,0},{3,1},{4,2},{5,3},{6,4},{7,5},{8,14},{9,15},{10,... | collective-permute-start | bytes 12296 | tf_op jit(solution)/shard_map/ppermute | solution.py:364
  5.8 4.7 %collective-permute-start.1 = (bf16[16,128]{1,0:T(8,128)(2,1)}, bf16[16,128]{1,0:T(8,128)(2,1)S(1)}, u32[]{:S(2)}, u32[]{:S(2)}) collective-permute-start(bf16[16,128]{1,0:T(8,128)(2,1)} %bitcast.8), channel_id=1, source_target_pairs={{0,4},{1,5},{2,6},{3,7},{4,0},{5,1},{6,2},{7,3},{8,12},{9,13},{10,... | collective-permute-start | bytes 12296 | tf_op jit(solution)/shard_map/ppermute | solution.py:364
  5.8 5.6 %collective-permute-start = (bf16[16,128]{1,0:T(8,128)(2,1)}, bf16[16,128]{1,0:T(8,128)(2,1)S(1)}, u32[]{:S(2)}, u32[]{:S(2)}) collective-permute-start(bf16[16,128]{1,0:T(8,128)(2,1)} %bitcast.9), channel_id=1, source_target_pairs={{0,2},{1,3},{2,4},{3,5},{4,6},{5,7},{6,0},{7,1},{8,10},{9,11},{10,... | collective-permute-start | bytes 12296 | tf_op jit(solution)/shard_map/ppermute | solution.py:364
  12.1 2.9 %copy-start = (bf16[8,64,128]{2,1,0:T(8,128)(2,1)S(1)}, bf16[8,64,128]{2,1,0:T(8,128)(2,1)}, u32[]{:S(2)}) copy-start(bf16[8,64,128]{2,1,0:T(8,128)(2,1)} %summary_keys_ref.3) | copy-start | bytes 393220
  12.1 2.9 %copy-start.1 = (bf16[8,64,128]{2,1,0:T(8,128)(2,1)S(1)}, bf16[8,64,128]{2,1,0:T(8,128)(2,1)}, u32[]{:S(2)}) copy-start(bf16[8,64,128]{2,1,0:T(8,128)(2,1)} %summary_values_ref.3) | copy-start | bytes 393220
  12.1 15.6 %copy-start.2 = (f32[2,4,4]{2,1,0:T(4,128)S(1)}, f32[2,4,4]{2,1,0:T(4,128)}, u32[]{:S(2)}) copy-start(f32[2,4,4]{2,1,0:T(4,128)} %refs_4_.1) | copy-start | bytes 388
  12.1 2.9 %collective-permute-start.3 = (bf16[4,16,128]{2,1,0:T(8,128)(2,1)S(1)}, bf16[4,16,128]{2,1,0:T(8,128)(2,1)S(1)}, u32[]{:S(2)}, u32[]{:S(2)}) collective-permute-start(bf16[4,16,128]{2,1,0:T(8,128)(2,1)S(1)} %pad_maximum_fusion.query_ref), channel_id=1, source_target_pairs={{0,1},{1,0},{2,3},{3,2},{4,5},{5,4},{6,7},{7,6},{8,9},{9,8},{10,11... | collective-permute-start | bytes 49160 | tf_op jit(solution)/shard_map/ppermute | solution.py:374
  16.4 4.0 %collective-permute-start.4 = (f32[4,48,128]{2,1,0:T(8,128)S(1)}, f32[4,48,128]{2,1,0:T(8,128)S(1)}, u32[]{:S(2)}, u32[]{:S(2)}) collective-permute-start(f32[4,48,128]{2,1,0:T(8,128)S(1)} %other_half.1), channel_id=1, source_target_pairs={{0,1},{1,0},{2,3},{3,2},{4,5},{5,4},{6,7},{7,6},{8,9},{9,8},{10,11... | collective-permute-start | bytes 294920 | tf_op jit(solution)/shard_map/ppermute | solution.py:377
  16.7 3.6 %collective-permute-start.5 = (bf16[8,128]{1,0:T(8,128)(2,1)S(1)}, bf16[8,128]{1,0:T(8,128)(2,1)S(1)}, u32[]{:S(2)}, u32[]{:S(2)}) collective-permute-start(bf16[8,128]{1,0:T(8,128)(2,1)S(1)} %get-tuple-element.13.refs_5_), channel_id=1, source_target_pairs={{8,0},{9,1},{18,2},{19,3},{12,4},{13,5},{30,6},{31,7},{0,8},{1,9},... | collective-permute-start | bytes 6152 | tf_op jit(solution)/shard_map/ppermute | solution.py:372
  20.7 3.8 %collective-permute-start.6 = (bf16[56,128]{1,0:T(8,128)(2,1)S(1)}, bf16[56,128]{1,0:T(8,128)(2,1)S(1)}, u32[]{:S(2)}, u32[]{:S(2)}) collective-permute-start(bf16[56,128]{1,0:T(8,128)(2,1)S(1)} %get-tuple-element.15), channel_id=1, source_target_pairs={{0,6},{1,7},{2,0},{3,1},{4,2},{5,3},{6,4},{7,5},{8,14},{9,15},{10,... | collective-permute-start | bytes 43016 | tf_op jit(solution)/shard_map/ppermute | solution.py:380
  22.2 4.7 %collective-permute-start.7 = (bf16[56,128]{1,0:T(8,128)(2,1)S(1)}, bf16[56,128]{1,0:T(8,128)(2,1)S(1)}, u32[]{:S(2)}, u32[]{:S(2)}) collective-permute-start(bf16[56,128]{1,0:T(8,128)(2,1)S(1)} %get-tuple-element.16), channel_id=1, source_target_pairs={{0,4},{1,5},{2,6},{3,7},{4,0},{5,1},{6,2},{7,3},{8,12},{9,13},{10,... | collective-permute-start | bytes 43016 | tf_op jit(solution)/shard_map/ppermute | solution.py:380
  22.2 5.5 %collective-permute-start.8 = (bf16[56,128]{1,0:T(8,128)(2,1)S(1)}, bf16[56,128]{1,0:T(8,128)(2,1)S(1)}, u32[]{:S(2)}, u32[]{:S(2)}) collective-permute-start(bf16[56,128]{1,0:T(8,128)(2,1)S(1)} %get-tuple-element.17), channel_id=1, source_target_pairs={{0,2},{1,3},{2,4},{3,5},{4,6},{5,7},{6,0},{7,1},{8,10},{9,11},{10,... | collective-permute-start | bytes 43016 | tf_op jit(solution)/shard_map/ppermute | solution.py:380
where the time goes:
time: 28.8 us; the launch traced here: 28.6 us
  starting transfers between devices  11.3 us (39%)
  waiting for transfers between devices  9.23 us (32%)
  Pallas kernels  6.67 us (23%)
  between operations  0.7 us (2%)
  other arithmetic  0.69 us (2%)
    ppermute x3, starting transfers between devices, by_chips(): arrived.append(lax.ppermute(mine, 'shard', shift(step)))  6.14 us
    ppermute x3, waiting for transfers between devices, by_chips(): arrived.append(lax.ppermute(mine, 'shard', shift(step)))  4.6 us
    ppermute x3, waiting for transfers between devices, by_chips(): parts[step] = lax.ppermute(parts[step], 'shard', shift(-step))  3.86 us
    ppermute x3, starting transfers between devices, by_chips(): parts[step] = lax.ppermute(parts[step], 'shard', shift(-step))  3.2 us
    pallas_call x1, Pallas kernels, fetch(): pl.pallas_call(functools.partial(fetch_kernel, slots_here=slots_here, blo...  2.82 us
    pallas_call x2, Pallas kernels, half(): pl.pallas_call(functools.partial(half_kernel, heads_here=heads_here, flip...  2.68 us
    ppermute x1, starting transfers between devices, by_chips(): told = lax.ppermute(counts, ('grp', 'shard'), pairs)  1.49 us
    pallas_call x1, Pallas kernels, finish(): pl.pallas_call(finish_kernel, out_shape=(jax.ShapeDtypeStruct((rows, widt...  0.85 us
  transfers between devices with their start and end apart: 9, of which 7 were waited for; matrix products, arithmetic and copies ran while one was open for 0% of the time, Pallas kernels for 15%

commit v1 on v0

--- a/solution.py
+++ b/solution.py
@@ -14,39 +14,43 @@
 LIMIT = 4 * 1024 * 1024
 
 
-def fetch_kernel(rows_hbm, picked_hbm, keys_hbm, values_hbm, keys_out, values_out, counts_out, *refs, slots_here, blocks_each):
-    valid_out = refs[0] if len(refs) == 9 else None
-    rows_ref, picked_ref, picked_tile, rows_sem, picked_sem, tile_sem, key_sem, value_sem = refs[-8:]
-    copies = [
-        pltpu.make_async_copy(rows_hbm, rows_ref, rows_sem),
-        pltpu.make_async_copy(picked_hbm, picked_ref, picked_sem),
-        pltpu.make_async_copy(picked_hbm, picked_tile, tile_sem),
-    ]
+def fetch_kernel(rows_hbm, picked_hbm, keys_hbm, values_hbm, keys_out, values_out, counts_out, *refs, slots_here, blocks_each, with_valid):
+    valid_out = refs[0] if with_valid else None
+    sequences, blocks = rows_hbm.shape
+    *rows_refs, picked_ref, picked_tile, rows_sem, picked_sem, tile_sem, key_sem, value_sem = refs[-7 - sequences :]
+    copies = [pltpu.make_async_copy(rows_hbm.at[i], ref, rows_sem.at[i]) for i, ref in enumerate(rows_refs)]
+    copies.append(pltpu.make_async_copy(picked_hbm, picked_ref, picked_sem))
+    copies.append(pltpu.make_async_copy(picked_hbm, picked_tile, tile_sem))
     for copy in copies:
         copy.start()
-    key_heads, sequences, picks = picked_ref.shape
+    key_heads, _, picks = picked_ref.shape
     first = lax.axis_index("shard") * slots_here
-    for copy in copies[:2]:
+    for copy in copies[:-1]:
         copy.wait()
     for head in range(key_heads):
         for sequence in range(sequences):
-            place = jnp.int32(sequence * blocks_each)
-            found = jnp.int32(0)
+            places = []
             for pick in range(picks):
-                slot = rows_ref[sequence, picked_ref[head, sequence, pick]] - first
-                here = (slot >= 0) & (slot < slots_here)
-                place = jnp.where(here, slot, place)
-                found = jnp.where(here, 1, found)
+                slot = rows_refs[sequence][picked_ref[head, sequence, pick]]
+                if slots_here & (slots_here - 1) == 0:
+                    places.append(slot ^ first)
+                else:
+                    places.append(jnp.where(slot >= first, slot - first, slots_here))
+            while len(places) > 1:
+                places = [functools.reduce(jnp.minimum, places[i : i + 2]) for i in range(0, len(places), 2)]
+            place = places[0]
             if valid_out is not None:
-                valid_out[head, sequence] = found
+                found = place < slots_here
+                valid_out[head, sequence] = found.astype(jnp.int32)
+                place = jnp.where(found, place, sequence * blocks_each)
             pltpu.make_async_copy(keys_hbm.at[place, head], keys_out.at[head, sequence], key_sem).start()
             pltpu.make_async_copy(values_hbm.at[place, head], values_out.at[head, sequence], value_sem).start()
-    copies[2].wait()
+    copies[-1].wait()
     told_rows, width = counts_out.shape
     counts = []
     for row in range(told_rows):
         sums = [jnp.zeros((sequences, width), jnp.float32) for _ in range(2)]
-        if row * width < rows_ref.shape[1]:
+        if row * width < blocks:
             block_ids = lax.broadcasted_iota(jnp.int32, (sequences, width), 1) + row * width
             for head in range(key_heads):
                 tile = picked_tile[head]
@@ -70,16 +74,15 @@
         out_shape.append(jax.ShapeDtypeStruct((key_heads, sequences), jnp.int32))
         out_specs.append(pl.BlockSpec(memory_space=SMEM))
     out = pl.pallas_call(
-        functools.partial(fetch_kernel, slots_here=slots_here, blocks_each=slots_here // sequences),
+        functools.partial(
+            fetch_kernel, slots_here=slots_here, blocks_each=slots_here // sequences, with_valid=not always
+        ),
         out_shape=out_shape,
         in_specs=[pl.BlockSpec(memory_space=pltpu.HBM)] * 4,
         out_specs=out_specs,
-        scratch_shapes=[
-            SMEM(block_group_row.shape, jnp.int32),
-            SMEM(picked.shape, jnp.int32),
-            VMEM(picked.shape, jnp.int32),
-        ]
-        + [pltpu.SemaphoreType.DMA] * 5,
+        scratch_shapes=[SMEM(block_group_row.shape[1:], jnp.int32)] * sequences
+        + [SMEM(picked.shape, jnp.int32), VMEM(picked.shape, jnp.int32), pltpu.SemaphoreType.DMA((sequences,))]
+        + [pltpu.SemaphoreType.DMA] * 4,
         cost_estimate=pl.CostEstimate(flops=0, transcendentals=0, bytes_accessed=2 * nbytes),
         compiler_params=pltpu.CompilerParams(vmem_limit_bytes=LIMIT),
         name="fetch",
@@ -231,6 +234,7 @@
     chips, rows, width = query_ref.shape
     _, sequences, tokens, _ = keys_ref.shape
     slots = summary_keys_ref.shape[1]
+    scaling = width**-0.5
     me = lax.axis_index("shard")
     chip, core = me // 2, me % 2
     if flip:
@@ -238,16 +242,34 @@
     usable_block = usable_for(rows, sequences * tokens, tokens, heads_here, sequences)
     usable_summary = usable_for(rows, slots, slots // sequences, heads_here, sequences)
     lane = lax.broadcasted_iota(jnp.int32, (rows, width), 1)
+    heads = [lax.rem(chip + (chips - step), chips) * 2 + core for step in range(chips)]
+    key_parts, value_parts = [], []
+    for head in heads:
+        key_parts += [summary_keys_ref[head], keys_ref[head].reshape(sequences * tokens, width)]
+        value_parts += [summary_values_ref[head], values_ref[head].reshape(sequences * tokens, width)]
+    scores = [
+        lax.dot_general(query_ref[i // 2], keys, (((1,), (1,)), ((), ())), preferred_element_type=jnp.float32)
+        for i, keys in enumerate(key_parts)
+    ]
+    scores = [
+        jnp.where(usable_block if i % 2 else usable_summary, score * scaling, VERY_NEGATIVE)
+        for i, score in enumerate(scores)
+    ]
+    tops = [jnp.max(score, axis=-1, keepdims=True) for score in scores]
+    exponents = [jnp.exp(score - top) for score, top in zip(scores, tops)]
+    numerators = [
+        lax.dot_general(
+            exponent.astype(jnp.bfloat16), values, (((1,), (0,)), ((), ())), preferred_element_type=jnp.float32
+        )
+        for exponent, values in zip(exponents, value_parts)
+    ]
+    totals = [jnp.sum(exponent, axis=-1, keepdims=True) for exponent in exponents]
     for step in range(chips):
-        head = lax.rem(chip + (chips - step), chips) * 2 + core
-        query = query_ref[step]
-        keys = keys_ref[head].reshape(sequences * tokens, width)
-        values = values_ref[head].reshape(sequences * tokens, width)
-        top_s, sum_s, num_s = attend_part(query, keys, values, usable_block, None)
-        top_l, sum_l, num_l = attend_part(query, summary_keys_ref[head], summary_values_ref[head], usable_summary, None)
-        stats = jnp.where(lane == 0, top_l, jnp.where(lane == 1, sum_l, jnp.where(lane == 2, top_s, sum_s)))
-        out_ref[step, :rows, :] = num_l
-        out_ref[step, rows : 2 * rows, :] = num_s
+        l, s = 2 * step, 2 * step + 1
+        stats = jnp.where(lane == 2, tops[s], totals[s])
+        stats = jnp.where(lane == 0, tops[l], jnp.where(lane == 1, totals[l], stats))
+        out_ref[step, :rows, :] = numerators[l]
+        out_ref[step, rows : 2 * rows, :] = numerators[s]
         out_ref[step, 2 * rows :, :] = stats
 
 
@@ -363,7 +385,7 @@
     for step in range(1, chips):
         arrived.append(lax.ppermute(mine, "shard", shift(step)))
     keys, values, counts, _ = fetch(block_group_row, picked, keys_cache, values_cache, True)
-    offsets = [groups - 1 if chip == groups - 1 else chip % (groups - 2) + 1 for chip in range(chips)] if groups > 2 else [1] * chips
+    offsets = [groups - 1 if chip == groups - 1 else chip + 1 if chip < groups - 2 else 1 for chip in range(chips)]
     pairs = [
         ((group ^ offsets[shard // 2]) * shards + shard, group * shards + shard)
         for group in range(groups)

time: 28.8 us -> 27.7 us (0.962)
  Pallas kernels: 6.67 us -> 4.55 us
  waiting for transfers between devices: 9.23 us -> 10.1 us
    pallas_call x2, Pallas kernels: 2.68 us -> 0.86 us  [half(): pl.pallas_call(functools.partial(half_kernel, heads_here=heads_here, flip...]
    ppermute x1, waiting for transfers between devices: 0.76 us -> 1.67 us  [by_chips(): told = lax.ppermute(counts, ('grp', 'shard'), pairs)]
    pallas_call x1, Pallas kernels: 2.82 us -> 2.51 us  [fetch(): pl.pallas_call(functools.partial(fetch_kernel, slots_here=slots_here, blo...]
  transfers between devices with their start and end apart: 9 -> 9, of which waited for: 7 -> 7; matrix products, arithmetic and copies ran while one was open for 0% -> 0% of each run, Pallas kernels for 15% -> 11%
where the time goes in v1:
time: 27.7 us; the launch traced here: 27.4 us
  starting transfers between devices  11.3 us (41%)
  waiting for transfers between devices  10.1 us (36%)
  Pallas kernels  4.55 us (16%)
  between operations  0.7 us (3%)
  other arithmetic  0.69 us (2%)
    ppermute x3, starting transfers between devices, by_chips(): arrived.append(lax.ppermute(mine, 'shard', shift(step)))  6.14 us
    ppermute x3, waiting for transfers between devices, by_chips(): arrived.append(lax.ppermute(mine, 'shard', shift(step)))  4.6 us
    ppermute x3, waiting for transfers between devices, by_chips(): parts[step] = lax.ppermute(parts[step], 'shard', shift(-step))  3.86 us
    ppermute x3, starting transfers between devices, by_chips(): parts[step] = lax.ppermute(parts[step], 'shard', shift(-step))  3.2 us
    pallas_call x1, Pallas kernels, fetch(): pl.pallas_call(functools.partial(fetch_kernel, slots_here=slots_here, blo...  2.51 us
    ppermute x1, waiting for transfers between devices, by_chips(): told = lax.ppermute(counts, ('grp', 'shard'), pairs)  1.67 us
    ppermute x1, starting transfers between devices, by_chips(): told = lax.ppermute(counts, ('grp', 'shard'), pairs)  1.49 us
    pallas_call x2, Pallas kernels, half(): pl.pallas_call(functools.partial(half_kernel, heads_here=heads_here, flip...  0.86 us
  transfers between devices with their start and end apart: 9, of which 7 were waited for; matrix products, arithmetic and copies ran while one was open for 0% of the time, Pallas kernels for 11%

profile of v1, /device:TPU:0, one launch (start us, length us, event | category | flops | bytes accessed | tf_op | source)
XLA Modules:
  0.0 27.4 jit_solution(14893609939807536339)
XLA Ops:
  0.6 5.1 %collective-permute-start.2 = (bf16[16,128]{1,0:T(8,128)(2,1)}, bf16[16,128]{1,0:T(8,128)(2,1)S(1)}, u32[]{:S(2)}, u32[]{:S(2)}) collective-permute-start(bf16[16,128]{1,0:T(8,128)(2,1)} %bitcast.7), channel_id=1, source_target_pairs={{0,6},{1,7},{2,0},{3,1},{4,2},{5,3},{6,4},{7,5},{8,14},{9,15},{10,... | collective-permute-start | bytes 12296 | tf_op jit(solution)/shard_map/ppermute | solution.py:386
  5.8 0.0 collective-permute-start.1
  5.8 1.0 %collective-permute-start = (bf16[16,128]{1,0:T(8,128)(2,1)}, bf16[16,128]{1,0:T(8,128)(2,1)S(1)}, u32[]{:S(2)}, u32[]{:S(2)}) collective-permute-start(bf16[16,128]{1,0:T(8,128)(2,1)} %bitcast.9), channel_id=1, source_target_pairs={{0,2},{1,3},{2,4},{3,5},{4,6},{5,7},{6,0},{7,1},{8,10},{9,11},{10,... | collective-permute-start | bytes 12296 | tf_op jit(solution)/shard_map/ppermute | solution.py:386
  6.8 0.5 %collective-permute-done.2 = bf16[16,128]{1,0:T(8,128)(2,1)S(1)} collective-permute-done((bf16[16,128]{1,0:T(8,128)(2,1)}, bf16[16,128]{1,0:T(8,128)(2,1)S(1)}, u32[]{:S(2)}, u32[]{:S(2)}) %collective-permute-start.2) | collective-permute-done | bytes 4128 | tf_op jit(solution)/shard_map/ppermute | solution.py:386
  7.3 3.2 %collective-permute-done.1 = bf16[16,128]{1,0:T(8,128)(2,1)S(1)} collective-permute-done((bf16[16,128]{1,0:T(8,128)(2,1)}, bf16[16,128]{1,0:T(8,128)(2,1)S(1)}, u32[]{:S(2)}, u32[]{:S(2)}) %collective-permute-start.1) | collective-permute-done | bytes 4128 | tf_op jit(solution)/shard_map/ppermute | solution.py:386
  10.5 0.9 %collective-permute-done = bf16[16,128]{1,0:T(8,128)(2,1)S(1)} collective-permute-done((bf16[16,128]{1,0:T(8,128)(2,1)}, bf16[16,128]{1,0:T(8,128)(2,1)S(1)}, u32[]{:S(2)}, u32[]{:S(2)}) %collective-permute-start) | collective-permute-done | bytes 4128 | tf_op jit(solution)/shard_map/ppermute | solution.py:386
  11.4 0.7 %pad_maximum_fusion.query_ref = bf16[4,16,128]{2,1,0:T(8,128)(2,1)S(1)} fusion(bf16[1,16,128]{2,1,0:T(8,128)(2,1)S(1)} %bitcast.11, bf16[1,16,128]{2,1,0:T(8,128)(2,1)S(1)} %bitcast.12, bf16[1,16,128]{2,1,0:T(8,128)(2,1)S(1)} %bitcast.13, bf16[1,16,128]{2,1,0:T(8,128)(2,1)} %bitcast.10), kind=kLoop, calls=%fused_computation | loop fusion | flops 24576 | bytes 32768 | tf_op jit(solution)/shard_map/stack | solution.py:395
  12.1 0.0 copy-start
  12.1 0.0 copy-start.1
  12.1 0.0 copy-start.2
  12.1 0.1 collective-permute-start.3
  12.2 2.5 %fetch.1 = (bf16[8,4,64,128]{3,2,1,0:T(8,128)(2,1)S(1)}, bf16[8,4,64,128]{3,2,1,0:T(8,128)(2,1)S(1)}, bf16[8,128]{1,0:T(8,128)(2,1)S(1)}) custom-call(s32[4,128]{1,0:T(4,128)} %rows_hbm.1, s32[8,4,8]{2,1,0:T(4,128)} %picked_hbm.1, bf16[64,8,64,128]{3,2,1,0:T(8,128)(2,1)} %keys_hbm.1, bf16[64,8,64,128]{3,2,1,0:T(8,128)(2,1)} %values_hbm.1), custom_call_target="tpu_custom_call" | custom-call | bytes 2097152 | tf_op jit(solution)/shard_map/fetch/pallas_call | solution.py:76
  14.7 0.0 collective-permute-done.3.query_ref
  14.7 0.0 copy-done
  14.7 0.0 copy-done.1
  14.7 0.4 %other_half.1 = f32[4,48,128]{2,1,0:T(8,128)S(1)} custom-call(bf16[4,16,128]{2,1,0:T(8,128)(2,1)S(1)} %collective-permute-done.3.query_ref, bf16[8,4,64,128]{3,2,1,0:T(8,128)(2,1)S(1)} %get-tuple-element.11.keys_ref, bf16[8,4,64,128]{3,2,1,0:T(8,128)(2,1)S(1)} %get-tuple-element.12.values_ref, bf16[8,64,128]{2,1,0:T(8,128)(2,1)S(1)} %copy-done, ...), custom_call_target="tpu_custom_call" | custom-call | flops 100000000 | bytes 1000000 | tf_op jit(solution)/shard_map/other_half/pallas_call | solution.py:278
  15.2 0.4 %collective-permute-start.4 = (f32[4,48,128]{2,1,0:T(8,128)S(1)}, f32[4,48,128]{2,1,0:T(8,128)S(1)}, u32[]{:S(2)}, u32[]{:S(2)}) collective-permute-start(f32[4,48,128]{2,1,0:T(8,128)S(1)} %other_half.1), channel_id=1, source_target_pairs={{0,1},{1,0},{2,3},{3,2},{4,5},{5,4},{6,7},{7,6},{8,9},{9,8},{10,11... | collective-permute-start | bytes 294920 | tf_op jit(solution)/shard_map/ppermute | solution.py:399
  15.6 1.5 %collective-permute-start.5 = (bf16[8,128]{1,0:T(8,128)(2,1)S(1)}, bf16[8,128]{1,0:T(8,128)(2,1)S(1)}, u32[]{:S(2)}, u32[]{:S(2)}) collective-permute-start(bf16[8,128]{1,0:T(8,128)(2,1)S(1)} %get-tuple-element.13.refs_5_), channel_id=1, source_target_pairs={{8,0},{9,1},{18,2},{19,3},{12,4},{13,5},{30,6},{31,7},{0,8},{1,9},... | collective-permute-start | bytes 6152 | tf_op jit(solution)/shard_map/ppermute | solution.py:394
  17.1 0.4 %own_half.1.own_ref = f32[4,48,128]{2,1,0:T(8,128)S(1)} custom-call(bf16[4,16,128]{2,1,0:T(8,128)(2,1)S(1)} %pad_maximum_fusion.query_ref, bf16[8,4,64,128]{3,2,1,0:T(8,128)(2,1)S(1)} %get-tuple-element.11.keys_ref, bf16[8,4,64,128]{3,2,1,0:T(8,128)(2,1)S(1)} %get-tuple-element.12.values_ref, bf16[8,64,128]{2,1,0:T(8,128)(2,1)S(1)} %copy-done, ...), custom_call_target="tpu_custom_call" | custom-call | flops 100000000 | bytes 1000000 | tf_op jit(solution)/shard_map/own_half/pallas_call | solution.py:278
  17.5 1.7 %collective-permute-done.5.told_ref = bf16[8,128]{1,0:T(8,128)(2,1)S(1)} collective-permute-done((bf16[8,128]{1,0:T(8,128)(2,1)S(1)}, bf16[8,128]{1,0:T(8,128)(2,1)S(1)}, u32[]{:S(2)}, u32[]{:S(2)}) %collective-permute-start.5) | collective-permute-done | bytes 2080 | tf_op jit(solution)/shard_map/ppermute | solution.py:394
  19.2 0.0 collective-permute-done.4.other_ref
  19.2 0.3 %join.1 = (bf16[56,128]{1,0:T(8,128)(2,1)S(1)}, bf16[56,128]{1,0:T(8,128)(2,1)S(1)}, bf16[56,128]{1,0:T(8,128)(2,1)S(1)}, bf16[56,128]{1,0:T(8,128)(2,1)S(1)}) custom-call(f32[4,48,128]{2,1,0:T(8,128)S(1)} %own_half.1.own_ref, f32[4,48,128]{2,1,0:T(8,128)S(1)} %collective-permute-done.4.other_ref, bf16[8,128]{1,0:T(8,128)(2,1)S(1)} %collective-permute-done.5.told_ref), custom_call_target="tpu_custom_call" | custom-call | tf_op jit(solution)/shard_map/join/pallas_call | solution.py:319
  19.5 1.5 %collective-permute-start.6 = (bf16[56,128]{1,0:T(8,128)(2,1)S(1)}, bf16[56,128]{1,0:T(8,128)(2,1)S(1)}, u32[]{:S(2)}, u32[]{:S(2)}) collective-permute-start(bf16[56,128]{1,0:T(8,128)(2,1)S(1)} %get-tuple-element.15), channel_id=1, source_target_pairs={{0,6},{1,7},{2,0},{3,1},{4,2},{5,3},{6,4},{7,5},{8,14},{9,15},{10,... | collective-permute-start | bytes 43016 | tf_op jit(solution)/shard_map/ppermute | solution.py:402
  21.0 0.0 collective-permute-start.7
  21.0 1.7 %collective-permute-start.8 = (bf16[56,128]{1,0:T(8,128)(2,1)S(1)}, bf16[56,128]{1,0:T(8,128)(2,1)S(1)}, u32[]{:S(2)}, u32[]{:S(2)}) collective-permute-start(bf16[56,128]{1,0:T(8,128)(2,1)S(1)} %get-tuple-element.17), channel_id=1, source_target_pairs={{0,2},{1,3},{2,4},{3,5},{4,6},{5,7},{6,0},{7,1},{8,10},{9,11},{10,... | collective-permute-start | bytes 43016 | tf_op jit(solution)/shard_map/ppermute | solution.py:402
  22.7 0.6 %collective-permute-done.6.refs_1_ = bf16[56,128]{1,0:T(8,128)(2,1)S(1)} collective-permute-done((bf16[56,128]{1,0:T(8,128)(2,1)S(1)}, bf16[56,128]{1,0:T(8,128)(2,1)S(1)}, u32[]{:S(2)}, u32[]{:S(2)}) %collective-permute-start.6) | collective-permute-done | bytes 14368 | tf_op jit(solution)/shard_map/ppermute | solution.py:402
  23.3 2.5 %collective-permute-done.7.refs_2_ = bf16[56,128]{1,0:T(8,128)(2,1)S(1)} collective-permute-done((bf16[56,128]{1,0:T(8,128)(2,1)S(1)}, bf16[56,128]{1,0:T(8,128)(2,1)S(1)}, u32[]{:S(2)}, u32[]{:S(2)}) %collective-permute-start.7) | collective-permute-done | bytes 14368 | tf_op jit(solution)/shard_map/ppermute | solution.py:402
  25.8 0.8 %collective-permute-done.8.refs_3_ = bf16[56,128]{1,0:T(8,128)(2,1)S(1)} collective-permute-done((bf16[56,128]{1,0:T(8,128)(2,1)S(1)}, bf16[56,128]{1,0:T(8,128)(2,1)S(1)}, u32[]{:S(2)}, u32[]{:S(2)}) %collective-permute-start.8) | collective-permute-done | bytes 14368 | tf_op jit(solution)/shard_map/ppermute | solution.py:402
  26.6 0.0 copy-done.2
  26.6 0.8 %finish.1 = (f32[16,128]{1,0:T(8,128)}, f32[1,128]{1,0:T(1,128)}) custom-call(bf16[56,128]{1,0:T(8,128)(2,1)S(1)} %get-tuple-element.14.refs_0_, bf16[56,128]{1,0:T(8,128)(2,1)S(1)} %collective-permute-done.6.refs_1_, bf16[56,128]{1,0:T(8,128)(2,1)S(1)} %collective-permute-done.7.refs_2_, bf16[56,128]{1,0:T(8,128)(2,1)S(1)} %collective-permute-done.8.refs_3_, ...), custom_call_target="tpu_custom_call" | custom-call | tf_op jit(solution)/shard_map/finish/pallas_call | solution.py:359
Async XLA Ops:
  0.6 6.7 %collective-permute-start.2 = (bf16[16,128]{1,0:T(8,128)(2,1)}, bf16[16,128]{1,0:T(8,128)(2,1)S(1)}, u32[]{:S(2)}, u32[]{:S(2)}) collective-permute-start(bf16[16,128]{1,0:T(8,128)(2,1)} %bitcast.7), channel_id=1, source_target_pairs={{0,6},{1,7},{2,0},{3,1},{4,2},{5,3},{6,4},{7,5},{8,14},{9,15},{10,... | collective-permute-start | bytes 12296 | tf_op jit(solution)/shard_map/ppermute | solution.py:386
  5.8 4.7 %collective-permute-start.1 = (bf16[16,128]{1,0:T(8,128)(2,1)}, bf16[16,128]{1,0:T(8,128)(2,1)S(1)}, u32[]{:S(2)}, u32[]{:S(2)}) collective-permute-start(bf16[16,128]{1,0:T(8,128)(2,1)} %bitcast.8), channel_id=1, source_target_pairs={{0,4},{1,5},{2,6},{3,7},{4,0},{5,1},{6,2},{7,3},{8,12},{9,13},{10,... | collective-permute-start | bytes 12296 | tf_op jit(solution)/shard_map/ppermute | solution.py:386
  5.8 5.6 %collective-permute-start = (bf16[16,128]{1,0:T(8,128)(2,1)}, bf16[16,128]{1,0:T(8,128)(2,1)S(1)}, u32[]{:S(2)}, u32[]{:S(2)}) collective-permute-start(bf16[16,128]{1,0:T(8,128)(2,1)} %bitcast.9), channel_id=1, source_target_pairs={{0,2},{1,3},{2,4},{3,5},{4,6},{5,7},{6,0},{7,1},{8,10},{9,11},{10,... | collective-permute-start | bytes 12296 | tf_op jit(solution)/shard_map/ppermute | solution.py:386
  12.1 2.6 %copy-start = (bf16[8,64,128]{2,1,0:T(8,128)(2,1)S(1)}, bf16[8,64,128]{2,1,0:T(8,128)(2,1)}, u32[]{:S(2)}) copy-start(bf16[8,64,128]{2,1,0:T(8,128)(2,1)} %summary_keys_ref.3) | copy-start | bytes 393220
  12.1 2.6 %copy-start.1 = (bf16[8,64,128]{2,1,0:T(8,128)(2,1)S(1)}, bf16[8,64,128]{2,1,0:T(8,128)(2,1)}, u32[]{:S(2)}) copy-start(bf16[8,64,128]{2,1,0:T(8,128)(2,1)} %summary_values_ref.3) | copy-start | bytes 393220
  12.1 14.5 %copy-start.2 = (f32[2,4,4]{2,1,0:T(4,128)S(1)}, f32[2,4,4]{2,1,0:T(4,128)}, u32[]{:S(2)}) copy-start(f32[2,4,4]{2,1,0:T(4,128)} %refs_4_.1) | copy-start | bytes 388
  12.1 2.6 %collective-permute-start.3 = (bf16[4,16,128]{2,1,0:T(8,128)(2,1)S(1)}, bf16[4,16,128]{2,1,0:T(8,128)(2,1)S(1)}, u32[]{:S(2)}, u32[]{:S(2)}) collective-permute-start(bf16[4,16,128]{2,1,0:T(8,128)(2,1)S(1)} %pad_maximum_fusion.query_ref), channel_id=1, source_target_pairs={{0,1},{1,0},{2,3},{3,2},{4,5},{5,4},{6,7},{7,6},{8,9},{9,8},{10,11... | collective-permute-start | bytes 49160 | tf_op jit(solution)/shard_map/ppermute | solution.py:396
  15.2 4.0 %collective-permute-start.4 = (f32[4,48,128]{2,1,0:T(8,128)S(1)}, f32[4,48,128]{2,1,0:T(8,128)S(1)}, u32[]{:S(2)}, u32[]{:S(2)}) collective-permute-start(f32[4,48,128]{2,1,0:T(8,128)S(1)} %other_half.1), channel_id=1, source_target_pairs={{0,1},{1,0},{2,3},{3,2},{4,5},{5,4},{6,7},{7,6},{8,9},{9,8},{10,11... | collective-permute-start | bytes 294920 | tf_op jit(solution)/shard_map/ppermute | solution.py:399
  15.6 3.6 %collective-permute-start.5 = (bf16[8,128]{1,0:T(8,128)(2,1)S(1)}, bf16[8,128]{1,0:T(8,128)(2,1)S(1)}, u32[]{:S(2)}, u32[]{:S(2)}) collective-permute-start(bf16[8,128]{1,0:T(8,128)(2,1)S(1)} %get-tuple-element.13.refs_5_), channel_id=1, source_target_pairs={{8,0},{9,1},{18,2},{19,3},{12,4},{13,5},{30,6},{31,7},{0,8},{1,9},... | collective-permute-start | bytes 6152 | tf_op jit(solution)/shard_map/ppermute | solution.py:394
  19.5 3.8 %collective-permute-start.6 = (bf16[56,128]{1,0:T(8,128)(2,1)S(1)}, bf16[56,128]{1,0:T(8,128)(2,1)S(1)}, u32[]{:S(2)}, u32[]{:S(2)}) collective-permute-start(bf16[56,128]{1,0:T(8,128)(2,1)S(1)} %get-tuple-element.15), channel_id=1, source_target_pairs={{0,6},{1,7},{2,0},{3,1},{4,2},{5,3},{6,4},{7,5},{8,14},{9,15},{10,... | collective-permute-start | bytes 43016 | tf_op jit(solution)/shard_map/ppermute | solution.py:402
  21.0 4.7 %collective-permute-start.7 = (bf16[56,128]{1,0:T(8,128)(2,1)S(1)}, bf16[56,128]{1,0:T(8,128)(2,1)S(1)}, u32[]{:S(2)}, u32[]{:S(2)}) collective-permute-start(bf16[56,128]{1,0:T(8,128)(2,1)S(1)} %get-tuple-element.16), channel_id=1, source_target_pairs={{0,4},{1,5},{2,6},{3,7},{4,0},{5,1},{6,2},{7,3},{8,12},{9,13},{10,... | collective-permute-start | bytes 43016 | tf_op jit(solution)/shard_map/ppermute | solution.py:402
  21.0 5.5 %collective-permute-start.8 = (bf16[56,128]{1,0:T(8,128)(2,1)S(1)}, bf16[56,128]{1,0:T(8,128)(2,1)S(1)}, u32[]{:S(2)}, u32[]{:S(2)}) collective-permute-start(bf16[56,128]{1,0:T(8,128)(2,1)S(1)} %get-tuple-element.17), channel_id=1, source_target_pairs={{0,2},{1,3},{2,4},{3,5},{4,6},{5,7},{6,0},{7,1},{8,10},{9,11},{10,... | collective-permute-start | bytes 43016 | tf_op jit(solution)/shard_map/ppermute | solution.py:402

commit v2 on v1

--- a/solution.py
+++ b/solution.py
@@ -242,7 +242,7 @@
     usable_block = usable_for(rows, sequences * tokens, tokens, heads_here, sequences)
     usable_summary = usable_for(rows, slots, slots // sequences, heads_here, sequences)
     lane = lax.broadcasted_iota(jnp.int32, (rows, width), 1)
-    heads = [lax.rem(chip + (chips - step), chips) * 2 + core for step in range(chips)]
+    heads = [lax.rem(chip + (chips - step), chips) * 2 + (1 - core if step else core) for step in range(chips)]
     key_parts, value_parts = [], []
     for head in heads:
         key_parts += [summary_keys_ref[head], keys_ref[head].reshape(sequences * tokens, width)]
@@ -377,7 +377,7 @@
     rows = sequences * heads_here
 
     def shift(step):
-        return [(s, (s // 2 + step) % chips * 2 + s % 2) for s in range(shards)]
+        return [(s, (s // 2 + step) % chips * 2 + 1 - s % 2) for s in range(shards)]
 
     partner = [(s, s ^ 1) for s in range(shards)]
     mine = queries.reshape(rows, width)
@@ -385,9 +385,9 @@
     for step in range(1, chips):
         arrived.append(lax.ppermute(mine, "shard", shift(step)))
     keys, values, counts, _ = fetch(block_group_row, picked, keys_cache, values_cache, True)
-    offsets = [groups - 1 if chip == groups - 1 else chip + 1 if chip < groups - 2 else 1 for chip in range(chips)]
+    offsets = [groups - 1 if chip == groups - 1 else (chip + 1) % (groups - 1) for chip in range(chips)]
     pairs = [
-        ((group ^ offsets[shard // 2]) * shards + shard, group * shards + shard)
+        ((group ^ offsets[shard // 2]) * shards + (shard if offsets[shard // 2] else shard ^ 1), group * shards + shard)
         for group in range(groups)
         for shard in range(shards)
     ]

time: 27.7 us -> 25.9 us (0.935)
  the two profiles are of different devices: /device:TPU:0 before, /device:TPU:1 now
where the time goes in v2:
time: 25.9 us; the launch traced here: 25.6 us
  waiting for transfers between devices  10.1 us (39%)
  starting transfers between devices  9.64 us (37%)
  Pallas kernels  4.55 us (18%)
  between operations  0.7 us (3%)
  other arithmetic  0.69 us (3%)
    ppermute x3, starting transfers between devices, by_chips(): arrived.append(lax.ppermute(mine, 'shard', shift(step)))  5.49 us
    ppermute x3, waiting for transfers between devices, by_chips(): parts[step] = lax.ppermute(parts[step], 'shard', shift(-step))  4.94 us
    ppermute x3, waiting for transfers between devices, by_chips(): arrived.append(lax.ppermute(mine, 'shard', shift(step)))  4.31 us
    pallas_call x1, Pallas kernels, fetch(): pl.pallas_call(functools.partial(fetch_kernel, slots_here=slots_here, blo...  2.51 us
    ppermute x3, starting transfers between devices, by_chips(): parts[step] = lax.ppermute(parts[step], 'shard', shift(-step))  2.46 us
    ppermute x1, starting transfers between devices, by_chips(): told = lax.ppermute(counts, ('grp', 'shard'), pairs)  1.21 us
    pallas_call x2, Pallas kernels, half(): pl.pallas_call(functools.partial(half_kernel, heads_here=heads_here, flip...  0.86 us
    pallas_call x1, Pallas kernels, finish(): pl.pallas_call(finish_kernel, out_shape=(jax.ShapeDtypeStruct((rows, widt...  0.85 us
  transfers between devices with their start and end apart: 9, of which 7 were waited for; matrix products, arithmetic and copies ran while one was open for 0% of the time, Pallas kernels for 11%

profile of v2, /device:TPU:1, one launch (start us, length us, event | category | flops | bytes accessed | tf_op | source)
XLA Modules:
  0.0 25.6 jit_solution(12504707076735730673)
XLA Ops:
  0.6 4.8 %collective-permute-start.2 = (bf16[16,128]{1,0:T(8,128)(2,1)}, bf16[16,128]{1,0:T(8,128)(2,1)S(1)}, u32[]{:S(2)}, u32[]{:S(2)}) collective-permute-start(bf16[16,128]{1,0:T(8,128)(2,1)} %bitcast.7), channel_id=1, source_target_pairs={{0,7},{1,6},{2,1},{3,0},{4,3},{5,2},{6,5},{7,4},{8,15},{9,14},{10,... | collective-permute-start | bytes 12296 | tf_op jit(solution)/shard_map/ppermute | solution.py:386
  5.4 0.0 collective-permute-start.1
  5.4 0.7 %collective-permute-start = (bf16[16,128]{1,0:T(8,128)(2,1)}, bf16[16,128]{1,0:T(8,128)(2,1)S(1)}, u32[]{:S(2)}, u32[]{:S(2)}) collective-permute-start(bf16[16,128]{1,0:T(8,128)(2,1)} %bitcast.9), channel_id=1, source_target_pairs={{0,3},{1,2},{2,5},{3,4},{4,7},{5,6},{6,1},{7,0},{8,11},{9,10},{10,... | collective-permute-start | bytes 12296 | tf_op jit(solution)/shard_map/ppermute | solution.py:386
  6.1 0.2 collective-permute-done.2
  6.3 3.5 %collective-permute-done.1 = bf16[16,128]{1,0:T(8,128)(2,1)S(1)} collective-permute-done((bf16[16,128]{1,0:T(8,128)(2,1)}, bf16[16,128]{1,0:T(8,128)(2,1)S(1)}, u32[]{:S(2)}, u32[]{:S(2)}) %collective-permute-start.1) | collective-permute-done | bytes 4128 | tf_op jit(solution)/shard_map/ppermute | solution.py:386
  9.8 0.6 %collective-permute-done = bf16[16,128]{1,0:T(8,128)(2,1)S(1)} collective-permute-done((bf16[16,128]{1,0:T(8,128)(2,1)}, bf16[16,128]{1,0:T(8,128)(2,1)S(1)}, u32[]{:S(2)}, u32[]{:S(2)}) %collective-permute-start) | collective-permute-done | bytes 4128 | tf_op jit(solution)/shard_map/ppermute | solution.py:386
  10.4 0.7 %pad_maximum_fusion.query_ref = bf16[4,16,128]{2,1,0:T(8,128)(2,1)S(1)} fusion(bf16[1,16,128]{2,1,0:T(8,128)(2,1)S(1)} %bitcast.11, bf16[1,16,128]{2,1,0:T(8,128)(2,1)S(1)} %bitcast.12, bf16[1,16,128]{2,1,0:T(8,128)(2,1)S(1)} %bitcast.13, bf16[1,16,128]{2,1,0:T(8,128)(2,1)} %bitcast.10), kind=kLoop, calls=%fused_computation | loop fusion | flops 24576 | bytes 32768 | tf_op jit(solution)/shard_map/stack | solution.py:395
  11.1 0.0 copy-start
  11.1 0.0 copy-start.1
  11.1 0.0 copy-start.2
  11.1 0.1 collective-permute-start.3
  11.2 2.5 %fetch.1 = (bf16[8,4,64,128]{3,2,1,0:T(8,128)(2,1)S(1)}, bf16[8,4,64,128]{3,2,1,0:T(8,128)(2,1)S(1)}, bf16[8,128]{1,0:T(8,128)(2,1)S(1)}) custom-call(s32[4,128]{1,0:T(4,128)} %rows_hbm.1, s32[8,4,8]{2,1,0:T(4,128)} %picked_hbm.1, bf16[64,8,64,128]{3,2,1,0:T(8,128)(2,1)} %keys_hbm.1, bf16[64,8,64,128]{3,2,1,0:T(8,128)(2,1)} %values_hbm.1), custom_call_target="tpu_custom_call" | custom-call | bytes 2097152 | tf_op jit(solution)/shard_map/fetch/pallas_call | solution.py:76
  13.7 0.0 collective-permute-done.3.query_ref
  13.7 0.0 copy-done
  13.8 0.0 copy-done.1
  13.8 0.4 %other_half.1 = f32[4,48,128]{2,1,0:T(8,128)S(1)} custom-call(bf16[4,16,128]{2,1,0:T(8,128)(2,1)S(1)} %collective-permute-done.3.query_ref, bf16[8,4,64,128]{3,2,1,0:T(8,128)(2,1)S(1)} %get-tuple-element.11.keys_ref, bf16[8,4,64,128]{3,2,1,0:T(8,128)(2,1)S(1)} %get-tuple-element.12.values_ref, bf16[8,64,128]{2,1,0:T(8,128)(2,1)S(1)} %copy-done, ...), custom_call_target="tpu_custom_call" | custom-call | flops 100000000 | bytes 1000000 | tf_op jit(solution)/shard_map/other_half/pallas_call | solution.py:278
  14.2 0.4 %collective-permute-start.4 = (f32[4,48,128]{2,1,0:T(8,128)S(1)}, f32[4,48,128]{2,1,0:T(8,128)S(1)}, u32[]{:S(2)}, u32[]{:S(2)}) collective-permute-start(f32[4,48,128]{2,1,0:T(8,128)S(1)} %other_half.1), channel_id=1, source_target_pairs={{0,1},{1,0},{2,3},{3,2},{4,5},{5,4},{6,7},{7,6},{8,9},{9,8},{10,11... | collective-permute-start | bytes 294920 | tf_op jit(solution)/shard_map/ppermute | solution.py:399
  14.6 1.2 %collective-permute-start.5 = (bf16[8,128]{1,0:T(8,128)(2,1)S(1)}, bf16[8,128]{1,0:T(8,128)(2,1)S(1)}, u32[]{:S(2)}, u32[]{:S(2)}) collective-permute-start(bf16[8,128]{1,0:T(8,128)(2,1)S(1)} %get-tuple-element.13.refs_5_), channel_id=1, source_target_pairs={{8,0},{9,1},{18,2},{19,3},{5,4},{4,5},{30,6},{31,7},{0,8},{1,9},{2... | collective-permute-start | bytes 6152 | tf_op jit(solution)/shard_map/ppermute | solution.py:394
  15.8 0.4 %own_half.1.own_ref = f32[4,48,128]{2,1,0:T(8,128)S(1)} custom-call(bf16[4,16,128]{2,1,0:T(8,128)(2,1)S(1)} %pad_maximum_fusion.query_ref, bf16[8,4,64,128]{3,2,1,0:T(8,128)(2,1)S(1)} %get-tuple-element.11.keys_ref, bf16[8,4,64,128]{3,2,1,0:T(8,128)(2,1)S(1)} %get-tuple-element.12.values_ref, bf16[8,64,128]{2,1,0:T(8,128)(2,1)S(1)} %copy-done, ...), custom_call_target="tpu_custom_call" | custom-call | flops 100000000 | bytes 1000000 | tf_op jit(solution)/shard_map/own_half/pallas_call | solution.py:278
  16.3 0.8 %collective-permute-done.5.told_ref = bf16[8,128]{1,0:T(8,128)(2,1)S(1)} collective-permute-done((bf16[8,128]{1,0:T(8,128)(2,1)S(1)}, bf16[8,128]{1,0:T(8,128)(2,1)S(1)}, u32[]{:S(2)}, u32[]{:S(2)}) %collective-permute-start.5) | collective-permute-done | bytes 2080 | tf_op jit(solution)/shard_map/ppermute | solution.py:394
  17.1 0.0 collective-permute-done.4.other_ref
  17.1 0.3 %join.1 = (bf16[56,128]{1,0:T(8,128)(2,1)S(1)}, bf16[56,128]{1,0:T(8,128)(2,1)S(1)}, bf16[56,128]{1,0:T(8,128)(2,1)S(1)}, bf16[56,128]{1,0:T(8,128)(2,1)S(1)}) custom-call(f32[4,48,128]{2,1,0:T(8,128)S(1)} %own_half.1.own_ref, f32[4,48,128]{2,1,0:T(8,128)S(1)} %collective-permute-done.4.other_ref, bf16[8,128]{1,0:T(8,128)(2,1)S(1)} %collective-permute-done.5.told_ref), custom_call_target="tpu_custom_call" | custom-call | tf_op jit(solution)/shard_map/join/pallas_call | solution.py:319
  17.4 2.5 %collective-permute-start.6 = (bf16[56,128]{1,0:T(8,128)(2,1)S(1)}, bf16[56,128]{1,0:T(8,128)(2,1)S(1)}, u32[]{:S(2)}, u32[]{:S(2)}) collective-permute-start(bf16[56,128]{1,0:T(8,128)(2,1)S(1)} %get-tuple-element.15), channel_id=1, source_target_pairs={{0,7},{1,6},{2,1},{3,0},{4,3},{5,2},{6,5},{7,4},{8,15},{9,14},{10,... | collective-permute-start | bytes 43016 | tf_op jit(solution)/shard_map/ppermute | solution.py:402
  19.8 0.0 collective-permute-start.7
  19.8 0.0 collective-permute-start.8
  19.9 0.8 %collective-permute-done.6.refs_1_ = bf16[56,128]{1,0:T(8,128)(2,1)S(1)} collective-permute-done((bf16[56,128]{1,0:T(8,128)(2,1)S(1)}, bf16[56,128]{1,0:T(8,128)(2,1)S(1)}, u32[]{:S(2)}, u32[]{:S(2)}) %collective-permute-start.6) | collective-permute-done | bytes 14368 | tf_op jit(solution)/shard_map/ppermute | solution.py:402
  20.7 3.3 %collective-permute-done.7.refs_2_ = bf16[56,128]{1,0:T(8,128)(2,1)S(1)} collective-permute-done((bf16[56,128]{1,0:T(8,128)(2,1)S(1)}, bf16[56,128]{1,0:T(8,128)(2,1)S(1)}, u32[]{:S(2)}, u32[]{:S(2)}) %collective-permute-start.7) | collective-permute-done | bytes 14368 | tf_op jit(solution)/shard_map/ppermute | solution.py:402
  24.0 0.8 %collective-permute-done.8.refs_3_ = bf16[56,128]{1,0:T(8,128)(2,1)S(1)} collective-permute-done((bf16[56,128]{1,0:T(8,128)(2,1)S(1)}, bf16[56,128]{1,0:T(8,128)(2,1)S(1)}, u32[]{:S(2)}, u32[]{:S(2)}) %collective-permute-start.8) | collective-permute-done | bytes 14368 | tf_op jit(solution)/shard_map/ppermute | solution.py:402
  24.8 0.0 copy-done.2
  24.8 0.8 %finish.1 = (f32[16,128]{1,0:T(8,128)}, f32[1,128]{1,0:T(1,128)}) custom-call(bf16[56,128]{1,0:T(8,128)(2,1)S(1)} %get-tuple-element.14.refs_0_, bf16[56,128]{1,0:T(8,128)(2,1)S(1)} %collective-permute-done.6.refs_1_, bf16[56,128]{1,0:T(8,128)(2,1)S(1)} %collective-permute-done.7.refs_2_, bf16[56,128]{1,0:T(8,128)(2,1)S(1)} %collective-permute-done.8.refs_3_, ...), custom_call_target="tpu_custom_call" | custom-call | tf_op jit(solution)/shard_map/finish/pallas_call | solution.py:359
Async XLA Ops:
  0.6 5.7 %collective-permute-start.2 = (bf16[16,128]{1,0:T(8,128)(2,1)}, bf16[16,128]{1,0:T(8,128)(2,1)S(1)}, u32[]{:S(2)}, u32[]{:S(2)}) collective-permute-start(bf16[16,128]{1,0:T(8,128)(2,1)} %bitcast.7), channel_id=1, source_target_pairs={{0,7},{1,6},{2,1},{3,0},{4,3},{5,2},{6,5},{7,4},{8,15},{9,14},{10,... | collective-permute-start | bytes 12296 | tf_op jit(solution)/shard_map/ppermute | solution.py:386
  5.4 4.4 %collective-permute-start.1 = (bf16[16,128]{1,0:T(8,128)(2,1)}, bf16[16,128]{1,0:T(8,128)(2,1)S(1)}, u32[]{:S(2)}, u32[]{:S(2)}) collective-permute-start(bf16[16,128]{1,0:T(8,128)(2,1)} %bitcast.8), channel_id=1, source_target_pairs={{0,5},{1,4},{2,7},{3,6},{4,1},{5,0},{6,3},{7,2},{8,13},{9,12},{10,... | collective-permute-start | bytes 12296 | tf_op jit(solution)/shard_map/ppermute | solution.py:386
  5.4 5.0 %collective-permute-start = (bf16[16,128]{1,0:T(8,128)(2,1)}, bf16[16,128]{1,0:T(8,128)(2,1)S(1)}, u32[]{:S(2)}, u32[]{:S(2)}) collective-permute-start(bf16[16,128]{1,0:T(8,128)(2,1)} %bitcast.9), channel_id=1, source_target_pairs={{0,3},{1,2},{2,5},{3,4},{4,7},{5,6},{6,1},{7,0},{8,11},{9,10},{10,... | collective-permute-start | bytes 12296 | tf_op jit(solution)/shard_map/ppermute | solution.py:386
  11.1 2.6 %copy-start = (bf16[8,64,128]{2,1,0:T(8,128)(2,1)S(1)}, bf16[8,64,128]{2,1,0:T(8,128)(2,1)}, u32[]{:S(2)}) copy-start(bf16[8,64,128]{2,1,0:T(8,128)(2,1)} %summary_keys_ref.3) | copy-start | bytes 393220
  11.1 2.6 %copy-start.1 = (bf16[8,64,128]{2,1,0:T(8,128)(2,1)S(1)}, bf16[8,64,128]{2,1,0:T(8,128)(2,1)}, u32[]{:S(2)}) copy-start(bf16[8,64,128]{2,1,0:T(8,128)(2,1)} %summary_values_ref.3) | copy-start | bytes 393220
  11.1 13.7 %copy-start.2 = (f32[2,4,4]{2,1,0:T(4,128)S(1)}, f32[2,4,4]{2,1,0:T(4,128)}, u32[]{:S(2)}) copy-start(f32[2,4,4]{2,1,0:T(4,128)} %refs_4_.1) | copy-start | bytes 388
  11.1 2.6 %collective-permute-start.3 = (bf16[4,16,128]{2,1,0:T(8,128)(2,1)S(1)}, bf16[4,16,128]{2,1,0:T(8,128)(2,1)S(1)}, u32[]{:S(2)}, u32[]{:S(2)}) collective-permute-start(bf16[4,16,128]{2,1,0:T(8,128)(2,1)S(1)} %pad_maximum_fusion.query_ref), channel_id=1, source_target_pairs={{0,1},{1,0},{2,3},{3,2},{4,5},{5,4},{6,7},{7,6},{8,9},{9,8},{10,11... | collective-permute-start | bytes 49160 | tf_op jit(solution)/shard_map/ppermute | solution.py:396
  14.2 2.8 %collective-permute-start.4 = (f32[4,48,128]{2,1,0:T(8,128)S(1)}, f32[4,48,128]{2,1,0:T(8,128)S(1)}, u32[]{:S(2)}, u32[]{:S(2)}) collective-permute-start(f32[4,48,128]{2,1,0:T(8,128)S(1)} %other_half.1), channel_id=1, source_target_pairs={{0,1},{1,0},{2,3},{3,2},{4,5},{5,4},{6,7},{7,6},{8,9},{9,8},{10,11... | collective-permute-start | bytes 294920 | tf_op jit(solution)/shard_map/ppermute | solution.py:399
  14.6 2.4 %collective-permute-start.5 = (bf16[8,128]{1,0:T(8,128)(2,1)S(1)}, bf16[8,128]{1,0:T(8,128)(2,1)S(1)}, u32[]{:S(2)}, u32[]{:S(2)}) collective-permute-start(bf16[8,128]{1,0:T(8,128)(2,1)S(1)} %get-tuple-element.13.refs_5_), channel_id=1, source_target_pairs={{8,0},{9,1},{18,2},{19,3},{5,4},{4,5},{30,6},{31,7},{0,8},{1,9},{2... | collective-permute-start | bytes 6152 | tf_op jit(solution)/shard_map/ppermute | solution.py:394
  17.4 3.3 %collective-permute-start.6 = (bf16[56,128]{1,0:T(8,128)(2,1)S(1)}, bf16[56,128]{1,0:T(8,128)(2,1)S(1)}, u32[]{:S(2)}, u32[]{:S(2)}) collective-permute-start(bf16[56,128]{1,0:T(8,128)(2,1)S(1)} %get-tuple-element.15), channel_id=1, source_target_pairs={{0,7},{1,6},{2,1},{3,0},{4,3},{5,2},{6,5},{7,4},{8,15},{9,14},{10,... | collective-permute-start | bytes 43016 | tf_op jit(solution)/shard_map/ppermute | solution.py:402
  19.8 4.2 %collective-permute-start.7 = (bf16[56,128]{1,0:T(8,128)(2,1)S(1)}, bf16[56,128]{1,0:T(8,128)(2,1)S(1)}, u32[]{:S(2)}, u32[]{:S(2)}) collective-permute-start(bf16[56,128]{1,0:T(8,128)(2,1)S(1)} %get-tuple-element.16), channel_id=1, source_target_pairs={{0,5},{1,4},{2,7},{3,6},{4,1},{5,0},{6,3},{7,2},{8,13},{9,12},{10,... | collective-permute-start | bytes 43016 | tf_op jit(solution)/shard_map/ppermute | solution.py:402
  19.8 4.9 %collective-permute-start.8 = (bf16[56,128]{1,0:T(8,128)(2,1)S(1)}, bf16[56,128]{1,0:T(8,128)(2,1)S(1)}, u32[]{:S(2)}, u32[]{:S(2)}) collective-permute-start(bf16[56,128]{1,0:T(8,128)(2,1)S(1)} %get-tuple-element.17), channel_id=1, source_target_pairs={{0,3},{1,2},{2,5},{3,4},{4,7},{5,6},{6,1},{7,0},{8,11},{9,10},{10,... | collective-permute-start | bytes 43016 | tf_op jit(solution)/shard_map/ppermute | solution.py:402
